TPU v7x, 32 devices: a whole 2x2x4 slice. The times are simulated.
32 devices in a mesh: groups: 1, patch: 32 (over z, y, x, core), level: 1.
Axes of the slice: x: 2, y: 2, z: 4, core: 2. Of those that a mesh axis runs over, the one named last changes fastest.
Arguments:
- layer_input: bfloat16 [1, 4096, 1536], P('groups', 'patch', 'level'), may hold values from -24 to 24, as said below
- cotangent: bfloat16 [1, 4096, 1536], P('groups', 'patch', 'level'), may hold values from -6 to 6
- neighbours: int32 [4096, 6], P('patch'), may hold values from 0 to 192, as said below
- boundary: int32 [32, 64], P('patch'), may hold values from 0 to 127, as said below
- gauge_index: int32 [4096, 6], P('patch'), may hold values from 0 to 1023
- gauge_angles: float32 [1024], replicated, may hold values from -3.140625 to 3.140625
- norm_gain: float32 [1536], replicated, may hold values from 0.5 to 1.5
- up_weight: bfloat16 [1536, 2048], P('patch', 'level'), may hold values from -0.15625 to 0.15625
- down_weight: bfloat16 [1536, 2048], P('patch', 'level'), may hold values from -0.125 to 0.125
- self_real: bfloat16 [32, 32], replicated, may hold values from -0.75 to 0.75
- self_imag: bfloat16 [32, 32], replicated, may hold values from -0.75 to 0.75
- near_real: bfloat16 [32, 32], replicated, may hold values from -1.5 to 1.5
- near_imag: bfloat16 [32, 32], replicated, may hold values from -1.5 to 1.5
Outputs:
- layer_grad: bfloat16 [1, 4096, 1536], P('groups', 'patch', 'level')
Inputs may be any that keep to these rules, and one draw needn't show every extreme that they name: `layer_input`: the layer input is a real field; rows and features carry differing scales. `neighbours`: entry i of a column's row refers to its patch's extended rows: i < 128 is the patch's own column i, then 32 boundary columns of the previous patch in the cycle, then 32 of the next one; 192 appears only in the last entry and marks an absent neighbour. `boundary`: row p holds 64 distinct local columns of patch p: the first 32 are seen by patch p - 1, the rest by patch p + 1 (patches form a cycle).
All inputs are finite; a program needn't handle non-finite values.
Results may differ from a plain program's by a relative error of at most 0.014.
Values may be sent and summed in bfloat16 or wider, within the bound.
No kernel may reach another device: no remote copies, remote signals or barrier semaphores. Data moves between devices by JAX's collectives and lax.ppermute only.
A program may use at most 64 MiB of HBM per device.

v0:
```python
import jax
import jax.numpy as jnp
from jax import lax
from jax.sharding import PartitionSpec as P

CH = 64


def padded(shard, sides, width):
    for axis, dim in sides:
        devices, length = (lax.axis_size(axis), shard.shape[dim])
        up = [(i, (i + 1) % devices) for i in range(devices)]
        down = [(j, i) for i, j in up]
        last = lax.slice_in_dim(shard, length - width, length, axis=dim)
        leading = lax.slice_in_dim(shard, 0, width, axis=dim)
        before = lax.ppermute(last, axis, up)
        after = lax.ppermute(leading, axis, down)
        shard = jnp.concatenate([before, shard, after], axis=dim)
    return shard


def real_form(real_part, imag_part):
    upper = jnp.concatenate([real_part, imag_part], axis=1)
    lower = jnp.concatenate([-imag_part, real_part], axis=1)
    return jnp.concatenate([upper, lower], axis=0)


def rotate_quarter(values, channels):
    shape = values.shape
    split = values.reshape(shape[:-1] + (shape[-1] // channels, 2, channels // 2))
    turned = jnp.stack([-split[..., 1, :], split[..., 0, :]], axis=-2)
    return turned.reshape(shape)


def per_level(values, form, channels):
    shape = values.shape
    split = values.reshape(shape[:-1] + (shape[-1] // channels, channels))
    result = jnp.einsum("bclw,wv->bclv", split, form, preferred_element_type=jnp.float32)
    return result.reshape(shape)


def mlp_back(columns_in, grads, norm_gain, up_mat, down_mat):
    values = columns_in.astype(jnp.float32)
    root_scale = lax.rsqrt(jnp.mean(values * values, axis=-1, keepdims=True) + 1e-05)
    normed = (values * root_scale * norm_gain).astype(jnp.bfloat16)
    pre_act = jnp.einsum("brw,wh->brh", normed, up_mat, preferred_element_type=jnp.float32)
    back_hidden = jnp.einsum("brw,wh->brh", grads, down_mat, preferred_element_type=jnp.float32)
    sigmoid_pre = jax.nn.sigmoid(pre_act)
    grad_pre = (back_hidden * sigmoid_pre * (1.0 + pre_act * (1.0 - sigmoid_pre))).astype(
        jnp.bfloat16
    )
    grad_normed = jnp.einsum("brh,wh->brw", grad_pre, up_mat, preferred_element_type=jnp.float32)
    mixed_mean = jnp.mean(norm_gain * grad_normed * values, axis=-1, keepdims=True)
    return (
        root_scale * norm_gain * grad_normed
        - values * root_scale * root_scale * root_scale * mixed_mean
    )


def per_device(
    layer_input,
    cotangent,
    neighbours,
    boundary,
    gauge_index,
    gauge_angles,
    norm_gain,
    up_weight,
    down_weight,
    self_real,
    self_imag,
    near_real,
    near_imag,
):
    samples, columns, width = layer_input.shape
    border = boundary.shape[1] // 2
    low_rows = boundary[0, :border]
    high_rows = boundary[0, border:]
    sent = jnp.stack([layer_input[:, low_rows], layer_input[:, high_rows]])
    cycle = padded(sent, (("patch", 0),), 1)
    extended = jnp.concatenate(
        [layer_input, cycle[0], cycle[3], jnp.zeros((samples, 1, width), jnp.bfloat16)], axis=1
    )
    sentinel = columns + 2 * border
    present = (neighbours < sentinel).astype(jnp.float32)
    edge_weight = present / jnp.sum(present, axis=1, keepdims=True)
    phase = gauge_angles[gauge_index]
    cosine = jnp.cos(phase)
    sine = jnp.sin(phase)
    near_form = real_form(near_real, near_imag)
    self_form = real_form(self_real, self_imag)
    gathered = jnp.zeros((samples, columns, width), jnp.float32)
    for entry in range(6):
        near = extended[:, neighbours[:, entry]].astype(jnp.float32)
        turned = rotate_quarter(near, CH)
        gathered = (
            gathered
            + (
                cosine[None, :, entry : entry + 1] * near
                + sine[None, :, entry : entry + 1] * turned
            )
            * edge_weight[None, :, entry : entry + 1]
        )
    gathered = gathered.astype(jnp.bfloat16)
    convolved = per_level(gathered, near_form, CH) + per_level(layer_input, self_form, CH)
    conv_out = (layer_input.astype(jnp.float32) + convolved).astype(jnp.bfloat16)
    conv_out = lax.optimization_barrier(conv_out)
    up_part, down_part = (
        lax.all_gather(up_weight, "patch", axis=0, tiled=True),
        lax.all_gather(down_weight, "patch", axis=0, tiled=True),
    )
    up_whole, down_whole = (
        lax.all_gather(up_part, "level", axis=1, tiled=True),
        lax.all_gather(down_part, "level", axis=1, tiled=True),
    )
    half_cols, half_grads = (
        lax.all_to_all(conv_out, "level", split_axis=1, concat_axis=2, tiled=True),
        lax.all_to_all(cotangent, "level", split_axis=1, concat_axis=2, tiled=True),
    )
    terms = mlp_back(half_cols, half_grads, norm_gain, up_whole, down_whole)
    column_grad = (half_grads.astype(jnp.float32) + terms).astype(jnp.bfloat16)
    grad_conv = lax.all_to_all(column_grad, "level", split_axis=2, concat_axis=1, tiled=True)
    grad_conv = lax.optimization_barrier(grad_conv)
    pulled = per_level(grad_conv, near_form.T, CH)
    own_back = per_level(grad_conv, self_form.T, CH)
    pulled_turn = rotate_quarter(pulled, CH)
    spread = jnp.zeros((samples, sentinel + 1, width), jnp.float32)
    for entry in range(6):
        edges = (
            cosine[None, :, entry : entry + 1] * pulled
            - sine[None, :, entry : entry + 1] * pulled_turn
        ) * edge_weight[None, :, entry : entry + 1]
        spread = spread.at[:, neighbours[:, entry]].add(edges)
    back_sent = jnp.stack(
        [spread[:, columns : columns + border], spread[:, columns + border : sentinel]]
    )
    back_cycle = padded(back_sent.astype(jnp.bfloat16), (("patch", 0),), 1).astype(back_sent.dtype)
    local_terms = (
        spread[:, :columns].at[:, low_rows].add(back_cycle[0]).at[:, high_rows].add(back_cycle[3])
    )
    return (grad_conv.astype(jnp.float32) + own_back + local_terms).astype(jnp.bfloat16)


def solution(mesh):
    in_specs = (
        P("groups", "patch", "level"),
        P("groups", "patch", "level"),
        P("patch", None),
        P("patch", None),
        P("patch", None),
        P(),
        P(),
        P("patch", "level"),
        P("patch", "level"),
        P(),
        P(),
        P(),
        P(),
    )
    out_specs = P("groups", "patch", "level")
    return jax.shard_map(
        per_device, mesh=mesh, in_specs=in_specs, out_specs=out_specs, check_vma=False
    )
```

profile of v0, /device:TPU:0, one launch (start us, length us, event | category | flops | bytes accessed | tf_op | source)
XLA Modules:
  0.0 208.6 jit_solution(11459584941339266616)
XLA Ops:
  8.8 1.8 gather_fusion.1
  11.8 6.0 %collective-permute-start.1 = (bf16[1,1,32,1536]{3,2,1,0:T(8,128)(2,1)S(1)}, bf16[1,1,32,1536]{3,2,1,0:T(8,128)(2,1)S(1)}, u32[]{:S(2)}, u32[]{:S(2)}) collective-permute-start(bf16[1,1,32,1536]{3,2,1,0:T(8,128)(2,1)S(1)} %bitcast.166), channel_id=1, source_target_pairs={{1,0},{2,1},{3,2},{4,3},{5,4},{6,5},{7,6},{8,7},{9,8},{10,9},{11,1... | collective-permute-start | bytes 294920 | tf_op jit(solution)/shard_map/ppermute | solution.py:17
  18.4 3.2 %gather_fusion = f32[768]{0:T(1024)S(1)} fusion(f32[1024]{0:T(1024)S(1)} %copy-done, s32[1024]{0:T(1024)S(1)} %pad_clamp_fusion.8), kind=kCustom, calls=%fused_computation | custom fusion | bytes 9216 | tf_op jit(solution)/shard_map/gather | solution.py:87
  24.1 1.1 slice_reduce_fusion.10
  25.8 1.3 convolution_bitcast_fusion
  29.5 1.6 gather_fusion.5
  31.2 1.2 copy.90
  32.3 1.6 gather_fusion.6
  34.0 2.1 copy.92
  36.0 1.6 gather_fusion.7
  37.7 2.1 copy.94
  39.7 1.6 gather_fusion.8
  41.4 2.1 copy.96
  43.8 1.0 copy-done.2
  45.0 1.0 copy-done.3
  46.1 1.0 copy-done.4
  48.4 1.1 convolution_add_fusion
  50.0 32.1 %all-gather.5.cloned.1.call-done = bf16[1536,2048]{1,0:T(8,128)(2,1)} async-done(((bf16[48,2048]{1,0:T(8,128)(2,1)}), bf16[1536,2048]{1,0:T(8,128)(2,1)}) %all-gather.5.cloned.1.call-update) | async-done | bytes 6291472 | tf_op jit(solution)/shard_map/all_gather | solution.py:109
  82.1 3.8 %fusion.53 = f32[128,2048]{1,0:T(8,128)S(1)} fusion(bf16[1536,2048]{1,0:T(8,128)(2,1)} %all-gather.5.cloned.1.call-done, bf16[1,128,1536]{2,1,0:T(8,128)(2,1)S(1)} %add_convert_fusion, f32[1536]{0:T(1024)S(1)} %copy-done.19, f32[128]{0:T(128)S(1)} %add_rsqrt_fusion), kind=kOutput, calls=%fused_computation.87 | convolution fusion | flops 806092800 | bytes 7739904 | tf_op jit(solution)/shard_map/brw,wh->brh/dot_general | solution.py:46
  86.0 66.7 %all-gather.3.cloned.1.call-done = bf16[1536,2048]{1,0:T(8,128)(2,1)} async-done(((bf16[48,2048]{1,0:T(8,128)(2,1)}), bf16[1536,2048]{1,0:T(8,128)(2,1)}) %all-gather.3.cloned.1.call-update) | async-done | bytes 6291472 | tf_op jit(solution)/shard_map/all_gather | solution.py:110
  152.7 8.2 %fusion.11 = (f32[128]{0:T(128)S(1)}, f32[128,1536]{1,0:T(8,128)S(1)}) fusion(bf16[1,128,1536]{2,1,0:T(8,128)(2,1)S(1)} %add_convert_fusion, f32[1536]{0:T(1024)S(1)} %copy-done.19, bf16[1536,2048]{1,0:T(8,128)(2,1)} %all-gather.5.cloned.1.call-done, bf16[1536,2048]{1,0:T(8,128)(2,1)} %all-gather.3.cloned.1.call-done, f32[128,2048]{1,0:T(8,128)S(1)} %fusion.53, ...), kind=kOutput, calls=%fused_computation.34 | convolution fusion | flops 1613758336 | bytes 15211008 | tf_op jit(solution)/shard_map/brh,wh->brw/dot_general | solution.py:52
  163.3 3.4 %scatter_custom_fusion = f32[193,1536]{1,0:T(8,128)} fusion(s32[128]{0:T(128)} %copy-done.65, f32[1,128,1536]{2,1,0:T(8,128)S(1)} %copy.113, f32[1,128,1536]{2,1,0:T(8,128)S(1)} %copy.112, f32[]{:T(128)} %constant.5.clone.1, f32[128]{0:T(128)S(1)} %copy-done.28, f32[128]{0:T(128)S(1)} %get-tuple-element.11, f32[128]{0:T(128)S(1)} %copy-done.26), kind=kCustom, calls=%fused_computation.54 | custom fusion | flops 983040 | bytes 2760704 | tf_op jit(solution)/shard_map/scatter-add | solution.py:133
  166.7 4.4 %scatter_custom_fusion.1 = f32[193,1536]{1,0:T(8,128)} fusion(f32[193,1536]{1,0:T(8,128)} %scatter_custom_fusion, s32[128]{0:T(128)} %copy-done.64, f32[1,128,1536]{2,1,0:T(8,128)S(1)} %copy.113, f32[1,128,1536]{2,1,0:T(8,128)S(1)} %copy.112, f32[128]{0:T(128)S(1)} %copy-done.58, f32[128]{0:T(128)S(1)} %copy-done.46, f32[128]{0:T(128)S(1)} %copy-done.48), kind=kCustom, calls=%fused_computation.52 | custom fusion | flops 983040 | bytes 2760192 | tf_op jit(solution)/shard_map/scatter-add | solution.py:133
  171.2 4.4 %scatter_custom_fusion.2 = f32[193,1536]{1,0:T(8,128)} fusion(f32[193,1536]{1,0:T(8,128)} %scatter_custom_fusion.1, s32[128]{0:T(128)} %copy-done.63, f32[1,128,1536]{2,1,0:T(8,128)S(1)} %copy.113, f32[1,128,1536]{2,1,0:T(8,128)S(1)} %copy.112, f32[128]{0:T(128)S(1)} %copy-done.56, f32[128]{0:T(128)S(1)} %copy-done.42, f32[128]{0:T(128)S(1)} %copy-done.44), kind=kCustom, calls=%fused_computation.50 | custom fusion | flops 983040 | bytes 2760192 | tf_op jit(solution)/shard_map/scatter-add | solution.py:133
  175.6 4.4 %scatter_custom_fusion.3 = f32[193,1536]{1,0:T(8,128)} fusion(f32[193,1536]{1,0:T(8,128)} %scatter_custom_fusion.2, s32[128]{0:T(128)} %copy-done.62, f32[1,128,1536]{2,1,0:T(8,128)S(1)} %copy.113, f32[1,128,1536]{2,1,0:T(8,128)S(1)} %copy.112, f32[128]{0:T(128)S(1)} %copy-done.54, f32[128]{0:T(128)S(1)} %copy-done.38, f32[128]{0:T(128)S(1)} %copy-done.40), kind=kCustom, calls=%fused_computation.48 | custom fusion | flops 983040 | bytes 2760192 | tf_op jit(solution)/shard_map/scatter-add | solution.py:133
  180.1 4.4 %scatter_custom_fusion.4 = f32[193,1536]{1,0:T(8,128)} fusion(f32[193,1536]{1,0:T(8,128)} %scatter_custom_fusion.3, s32[128]{0:T(128)} %copy-done.61, f32[1,128,1536]{2,1,0:T(8,128)S(1)} %copy.113, f32[1,128,1536]{2,1,0:T(8,128)S(1)} %copy.112, f32[128]{0:T(128)S(1)} %copy-done.52, f32[128]{0:T(128)S(1)} %copy-done.34, f32[128]{0:T(128)S(1)} %copy-done.36), kind=kCustom, calls=%fused_computation.46 | custom fusion | flops 983040 | bytes 2760192 | tf_op jit(solution)/shard_map/scatter-add | solution.py:133
  184.5 4.4 %scatter_custom_fusion.5 = f32[193,1536]{1,0:T(8,128)} fusion(f32[193,1536]{1,0:T(8,128)} %scatter_custom_fusion.4, s32[128]{0:T(128)} %copy-done.60, f32[1,128,1536]{2,1,0:T(8,128)S(1)} %copy.113, f32[1,128,1536]{2,1,0:T(8,128)S(1)} %copy.112, f32[128]{0:T(128)S(1)} %copy-done.50, f32[128]{0:T(128)S(1)} %copy-done.30, f32[128]{0:T(128)S(1)} %copy-done.32), kind=kCustom, calls=%fused_computation.44 | custom fusion | flops 983040 | bytes 2760192 | tf_op jit(solution)/shard_map/scatter-add | solution.py:133
  188.9 1.1 fusion.102
  190.8 5.1 %collective-permute-start.3 = (bf16[1,1,32,1536]{3,2,1,0:T(8,128)(2,1)S(1)}, bf16[1,1,32,1536]{3,2,1,0:T(8,128)(2,1)S(1)}, u32[]{:S(2)}, u32[]{:S(2)}) collective-permute-start(bf16[1,1,32,1536]{3,2,1,0:T(8,128)(2,1)S(1)} %bitcast.161), channel_id=1, source_target_pairs={{1,0},{2,1},{3,2},{4,3},{5,4},{6,5},{7,6},{8,7},{9,8},{10,9},{11,1... | collective-permute-start | bytes 294920 | tf_op jit(solution)/shard_map/ppermute | solution.py:17
  196.0 2.3 %collective-permute-done.2 = bf16[1,1,32,1536]{3,2,1,0:T(8,128)(2,1)S(1)} collective-permute-done((bf16[1,1,32,1536]{3,2,1,0:T(8,128)(2,1)S(1)}, bf16[1,1,32,1536]{3,2,1,0:T(8,128)(2,1)S(1)}, u32[]{:S(2)}, u32[]{:S(2)}) %collective-permute-start.2) | collective-permute-done | bytes 98336 | tf_op jit(solution)/shard_map/ppermute | solution.py:16
  198.2 1.3 scatter_custom_fusion.6
  199.6 1.4 scatter_custom_fusion.7
  (201 shorter events, 15.3 us)
Async XLA Ops:
  6.5 11.8 %copy-start = (f32[1024]{0:T(1024)S(1)}, f32[1024]{0:T(1024)}, u32[]{:S(2)}) copy-start(f32[1024]{0:T(1024)} %param.18) | copy-start | bytes 12292
  6.5 4.6 %copy-start.1 = (bf16[1,128,1536]{2,1,0:T(8,128)(2,1)S(1)}, bf16[1,128,1536]{2,1,0:T(8,128)(2,1)}, u32[]{:S(2)}) copy-start(bf16[1,128,1536]{2,1,0:T(8,128)(2,1)} %param.13) | copy-start | bytes 1179652
  6.5 75.6 %all-gather.5.cloned.1.call-start = ((), (), s32[]{:S(2)}) async-start(), calls=%async_computation.1 | async-start | bytes 6488064 | tf_op jit(solution)/shard_map/all_gather | solution.py:109
  7.3 145.4 %all-gather.3.cloned.1.call-start = ((), (), s32[]{:S(2)}) async-start(), calls=%async_computation | async-start | bytes 6488064 | tf_op jit(solution)/shard_map/all_gather | solution.py:110
  8.8 9.2 %copy-start.59 = (s32[128,6]{0,1:T(8,128)S(1)}, s32[128,6]{0,1:T(8,128)}, u32[]{:S(2)}) copy-start(s32[128,6]{0,1:T(8,128)} %param.17) | copy-start | bytes 9220
  10.6 16.5 %collective-permute-start = (bf16[1,1,32,1536]{3,2,1,0:T(8,128)(2,1)S(1)}, bf16[1,1,32,1536]{3,2,1,0:T(8,128)(2,1)S(1)}, u32[]{:S(2)}, u32[]{:S(2)}) collective-permute-start(bf16[1,1,32,1536]{3,2,1,0:T(8,128)(2,1)S(1)} %bitcast.164), channel_id=1, source_target_pairs={{0,1},{1,2},{2,3},{3,4},{4,5},{5,6},{6,7},{7,8},{8,9},{9,10},{10,1... | collective-permute-start | bytes 294920 | tf_op jit(solution)/shard_map/ppermute | solution.py:16
  11.8 15.3 %collective-permute-start.1 = (bf16[1,1,32,1536]{3,2,1,0:T(8,128)(2,1)S(1)}, bf16[1,1,32,1536]{3,2,1,0:T(8,128)(2,1)S(1)}, u32[]{:S(2)}, u32[]{:S(2)}) collective-permute-start(bf16[1,1,32,1536]{3,2,1,0:T(8,128)(2,1)S(1)} %bitcast.166), channel_id=1, source_target_pairs={{1,0},{2,1},{3,2},{4,3},{5,4},{6,5},{7,6},{8,7},{9,8},{10,9},{11,1... | collective-permute-start | bytes 294920 | tf_op jit(solution)/shard_map/ppermute | solution.py:17
  18.4 3.8 %copy-start.23 = (bf16[32,32]{1,0:T(8,128)(2,1)S(1)}, bf16[32,32]{1,0:T(8,128)(2,1)}, u32[]{:S(2)}) copy-start(bf16[32,32]{1,0:T(8,128)(2,1)} %param.25) | copy-start | bytes 6148
  18.4 4.5 %copy-start.24 = (bf16[32,32]{1,0:T(8,128)(2,1)S(1)}, bf16[32,32]{1,0:T(8,128)(2,1)}, u32[]{:S(2)}) copy-start(bf16[32,32]{1,0:T(8,128)(2,1)} %param.24) | copy-start | bytes 6148
  18.4 5.2 %copy-start.20 = (s32[128,6]{0,1:T(8,128)S(1)}, s32[128,6]{0,1:T(8,128)}, u32[]{:S(2)}) copy-start(s32[128,6]{0,1:T(8,128)} %param.15) | copy-start | bytes 9220
  22.0 5.3 %copy-start.11 = (bf16[32,32]{0,1:T(8,128)(2,1)}, bf16[32,32]{0,1:T(8,128)(2,1)S(1)}, u32[]{:S(2)}) copy-start(bf16[32,32]{0,1:T(8,128)(2,1)S(1)} %neg.59) | copy-start | bytes 6148
  22.1 5.2 %copy-start.13 = (bf16[32,32]{0,1:T(8,128)(2,1)}, bf16[32,32]{0,1:T(8,128)(2,1)S(1)}, u32[]{:S(2)}) copy-start(bf16[32,32]{0,1:T(8,128)(2,1)S(1)} %copy.102) | copy-start | bytes 6148
  22.2 5.1 %copy-start.8 = (bf16[32,32]{0,1:T(8,128)(2,1)}, bf16[32,32]{0,1:T(8,128)(2,1)S(1)}, u32[]{:S(2)}) copy-start(bf16[32,32]{0,1:T(8,128)(2,1)S(1)} %copy.99) | copy-start | bytes 6148
  23.6 3.7 %copy-start.60 = (s32[128]{0:T(128)}, s32[128]{0:T(128)S(1)}, u32[]{:S(2)}) copy-start(s32[128]{0:T(128)S(1)} %get-tuple-element.47) | copy-start | bytes 1540
  23.6 3.7 %copy-start.61 = (s32[128]{0:T(128)}, s32[128]{0:T(128)S(1)}, u32[]{:S(2)}) copy-start(s32[128]{0:T(128)S(1)} %get-tuple-element.48) | copy-start | bytes 1540
  23.6 3.7 %copy-start.63 = (s32[128]{0:T(128)}, s32[128]{0:T(128)S(1)}, u32[]{:S(2)}) copy-start(s32[128]{0:T(128)S(1)} %get-tuple-element.45) | copy-start | bytes 1540
  49.8 32.4 %copy-start.19 = (f32[1536]{0:T(1024)S(1)}, f32[1536]{0:T(1024)}, u32[]{:S(2)}) copy-start(f32[1536]{0:T(1024)} %param.19) | copy-start | bytes 18436
  50.0 102.7 %copy-start.7 = (bf16[1,128,1536]{2,1,0:T(8,128)(2,1)S(1)}, bf16[1,128,1536]{2,1,0:T(8,128)(2,1)}, u32[]{:S(2)}) copy-start(bf16[1,128,1536]{2,1,0:T(8,128)(2,1)} %param.14) | copy-start | bytes 1179652
  166.7 4.5 %copy-start.42 = (f32[128]{0:T(128)S(1)}, f32[128]{0:T(128)}, u32[]{:S(2)}) copy-start(f32[128]{0:T(128)} %get-tuple-element.15) | copy-start | bytes 1540
  166.7 4.4 %copy-start.44 = (f32[128]{0:T(128)S(1)}, f32[128]{0:T(128)}, u32[]{:S(2)}) copy-start(f32[128]{0:T(128)} %get-tuple-element.62) | copy-start | bytes 1540
  166.7 4.4 %copy-start.56 = (f32[128]{0:T(128)S(1)}, f32[128]{0:T(128)}, u32[]{:S(2)}) copy-start(f32[128]{0:T(128)} %get-tuple-element.39) | copy-start | bytes 1540
  171.1 4.5 %copy-start.38 = (f32[128]{0:T(128)S(1)}, f32[128]{0:T(128)}, u32[]{:S(2)}) copy-start(f32[128]{0:T(128)} %get-tuple-element.14) | copy-start | bytes 1540
  171.2 4.4 %copy-start.40 = (f32[128]{0:T(128)S(1)}, f32[128]{0:T(128)}, u32[]{:S(2)}) copy-start(f32[128]{0:T(128)} %get-tuple-element.63) | copy-start | bytes 1540
  171.2 4.4 %copy-start.54 = (f32[128]{0:T(128)S(1)}, f32[128]{0:T(128)}, u32[]{:S(2)}) copy-start(f32[128]{0:T(128)} %get-tuple-element.38) | copy-start | bytes 1540
  175.6 4.5 %copy-start.34 = (f32[128]{0:T(128)S(1)}, f32[128]{0:T(128)}, u32[]{:S(2)}) copy-start(f32[128]{0:T(128)} %get-tuple-element.13) | copy-start | bytes 1540
  175.6 4.4 %copy-start.36 = (f32[128]{0:T(128)S(1)}, f32[128]{0:T(128)}, u32[]{:S(2)}) copy-start(f32[128]{0:T(128)} %get-tuple-element.64) | copy-start | bytes 1540
  175.6 4.4 %copy-start.52 = (f32[128]{0:T(128)S(1)}, f32[128]{0:T(128)}, u32[]{:S(2)}) copy-start(f32[128]{0:T(128)} %get-tuple-element.37) | copy-start | bytes 1540
  180.1 4.5 %copy-start.30 = (f32[128]{0:T(128)S(1)}, f32[128]{0:T(128)}, u32[]{:S(2)}) copy-start(f32[128]{0:T(128)} %get-tuple-element.12) | copy-start | bytes 1540
  180.1 4.4 %copy-start.32 = (f32[128]{0:T(128)S(1)}, f32[128]{0:T(128)}, u32[]{:S(2)}) copy-start(f32[128]{0:T(128)} %get-tuple-element.65) | copy-start | bytes 1540
  180.1 4.4 %copy-start.50 = (f32[128]{0:T(128)S(1)}, f32[128]{0:T(128)}, u32[]{:S(2)}) copy-start(f32[128]{0:T(128)} %get-tuple-element.36) | copy-start | bytes 1540
  190.5 7.7 %collective-permute-start.2 = (bf16[1,1,32,1536]{3,2,1,0:T(8,128)(2,1)S(1)}, bf16[1,1,32,1536]{3,2,1,0:T(8,128)(2,1)S(1)}, u32[]{:S(2)}, u32[]{:S(2)}) collective-permute-start(bf16[1,1,32,1536]{3,2,1,0:T(8,128)(2,1)S(1)} %bitcast.162), channel_id=1, source_target_pairs={{0,1},{1,2},{2,3},{3,4},{4,5},{5,6},{6,7},{7,8},{8,9},{9,10},{10,1... | collective-permute-start | bytes 294920 | tf_op jit(solution)/shard_map/ppermute | solution.py:16
  190.8 7.4 %collective-permute-start.3 = (bf16[1,1,32,1536]{3,2,1,0:T(8,128)(2,1)S(1)}, bf16[1,1,32,1536]{3,2,1,0:T(8,128)(2,1)S(1)}, u32[]{:S(2)}, u32[]{:S(2)}) collective-permute-start(bf16[1,1,32,1536]{3,2,1,0:T(8,128)(2,1)S(1)} %bitcast.161), channel_id=1, source_target_pairs={{1,0},{2,1},{3,2},{4,3},{5,4},{6,5},{7,6},{8,7},{9,8},{10,9},{11,1... | collective-permute-start | bytes 294920 | tf_op jit(solution)/shard_map/ppermute | solution.py:17
  (42 other events, 58.5 us)
Sparse Core Ops, SparseCore 0:
  10.2 71.8 all-gather.4
  85.0 67.6 all-gather.2
where the time goes:
time: 209 us
  waiting for transfers between devices  103 us (49%)
  local copies, waits for them, and re-layouts  32.3 us (15%)
  other arithmetic  32.2 us (15%)
  matrix products  15.2 us (7%)
  between operations  14.4 us (7%)
  starting transfers between devices  12 us (6%)
    all_gather x1, waiting for transfers between devices, per_device(): lax.all_gather(down_weight, 'patch', axis=0, tiled=True)  66.7 us
    all_gather x1, waiting for transfers between devices, per_device(): lax.all_gather(up_weight, 'patch', axis=0, tiled=True)  32.1 us
    scatter-add x6, other arithmetic, per_device(): spread = spread.at[:, neighbours[:, entry]].add(edges)  25.5 us
    ppermute x2, starting transfers between devices, padded(): after = lax.ppermute(leading, axis, down)  11.1 us
    gather x6, local copies, waits for them, and re-layouts, per_device(): near = extended[:, neighbours[:, entry]].astype(jnp.float32)  8.36 us
    dot_general x1, matrix products, mlp_back(): jnp.einsum('brh,wh->brw', grad_pre, up_mat, preferred_element_type=jnp.fl...  8.23 us
    convert_element_type x6, local copies, waits for them, and re-layouts, per_device(): near = extended[:, neighbours[:, entry]].astype(jnp.float32)  7.69 us
    unnamed x141, local copies, waits for them, and re-layouts  5.98 us
  transfers between devices with their start and end apart: 6, of which 3 were waited for; matrix products, arithmetic and copies ran while one was open for 16% of the time, Pallas kernels for 0%

commit v1 on v0

--- a/solution.py
+++ b/solution.py
@@ -4,6 +4,18 @@
 from jax.sharding import PartitionSpec as P
 
 CH = 64
+
+
+def gather_by_bits(x, axis, dim):
+    ways, here, hop = (lax.axis_size(axis), lax.axis_index(axis), x.shape[dim])
+    line, have = (x, 1)
+    while have < ways:
+        line = jnp.concatenate(
+            [line, lax.ppermute(line, axis, [(d, (d - have) % ways) for d in range(ways)])],
+            axis=dim,
+        )
+        have = 2 * have
+    return jnp.roll(line, here * hop, axis=dim)
 
 
 def padded(shard, sides, width):
@@ -107,7 +119,7 @@
     conv_out = lax.optimization_barrier(conv_out)
     up_part, down_part = (
         lax.all_gather(up_weight, "patch", axis=0, tiled=True),
-        lax.all_gather(down_weight, "patch", axis=0, tiled=True),
+        gather_by_bits(down_weight, "patch", 0),
     )
     up_whole, down_whole = (
         lax.all_gather(up_part, "level", axis=1, tiled=True),

time: 209 us -> 344 us (1.65)
  waiting for transfers between devices: 103 us -> 191 us
  local copies, waits for them, and re-layouts: 32.3 us -> 55.1 us
  starting transfers between devices: 12 us -> 23 us
  other arithmetic: 32.2 us -> 39.3 us
  matrix products: 15.2 us -> 20 us
    ppermute x0 -> x5, waiting for transfers between devices: none -> 188 us  [gather_by_bits(): lax.ppermute(line, axis, [(d, (d - have) % ways) for d in range(ways)])]
    all_gather x1 -> x0, waiting for transfers between devices: 66.7 us -> none  [per_device(): lax.all_gather(down_weight, 'patch', axis=0, tiled=True)]
    all_gather x1, waiting for transfers between devices: 32.1 us -> 0.01 us  [per_device(): lax.all_gather(up_weight, 'patch', axis=0, tiled=True)]
    unnamed x141 -> x165, local copies, waits for them, and re-layouts: 5.98 us -> 18.4 us
    concatenate x0 -> x2, local copies, waits for them, and re-layouts: none -> 7.57 us  [the longest x1 4.03 us: gather_by_bits(): return jnp.roll(line, here * hop, axis=dim)]
    ppermute x0 -> x5, starting transfers between devices: none -> 6.81 us  [gather_by_bits(): lax.ppermute(line, axis, [(d, (d - have) % ways) for d in range(ways)])]
    ppermute x2, starting transfers between devices: 11.1 us -> 16.1 us  [padded(): after = lax.ppermute(leading, axis, down)]
  transfers between devices with their start and end apart: 6 -> 10, of which waited for: 3 -> 5; matrix products, arithmetic and copies ran while one was open for 16% -> 18% of each run, Pallas kernels for 0% -> 0%
where the time goes in v1:
time: 344 us; the launch traced here: 343 us
  waiting for transfers between devices  191 us (56%)
  local copies, waits for them, and re-layouts  55.1 us (16%)
  other arithmetic  39.3 us (11%)
  starting transfers between devices  23 us (7%)
  matrix products  20 us (6%)
  between operations  14.5 us (4%)
    ppermute x5, waiting for transfers between devices, gather_by_bits(): lax.ppermute(line, axis, [(d, (d - have) % ways) for d in range(ways)])  188 us
    scatter-add x6, other arithmetic, per_device(): spread = spread.at[:, neighbours[:, entry]].add(edges)  25.5 us
    unnamed x165, local copies, waits for them, and re-layouts  18.4 us
    ppermute x2, starting transfers between devices, padded(): after = lax.ppermute(leading, axis, down)  16.1 us
    dot_general x1, matrix products, mlp_back(): jnp.einsum('brh,wh->brw', grad_pre, up_mat, preferred_element_type=jnp.fl...  11.5 us
    gather x6, local copies, waits for them, and re-layouts, per_device(): near = extended[:, neighbours[:, entry]].astype(jnp.float32)  9.1 us
    convert_element_type x6, local copies, waits for them, and re-layouts, per_device(): near = extended[:, neighbours[:, entry]].astype(jnp.float32)  8.73 us
  transfers between devices with their start and end apart: 10, of which 5 were waited for; matrix products, arithmetic and copies ran while one was open for 18% of the time, Pallas kernels for 0%

profile of v1, /device:TPU:0, one launch (start us, length us, event | category | flops | bytes accessed | tf_op | source)
XLA Modules:
  0.0 343.3 jit_solution(8593800781094205047)
XLA Ops:
  7.3 6.5 %collective-permute-start.2 = (bf16[48,2048]{1,0:T(8,128)(2,1)}, bf16[48,2048]{1,0:T(8,128)(2,1)S(1)}, u32[]{:S(2)}, u32[]{:S(2)}) collective-permute-start(bf16[48,2048]{1,0:T(8,128)(2,1)} %param.21), channel_id=1, source_target_pairs={{0,31},{1,0},{2,1},{3,2},{4,3},{5,4},{6,5},{7,6},{8,7},{9,8},{10,9... | collective-permute-start | bytes 589832 | tf_op jit(solution)/shard_map/ppermute | solution.py:14
  14.5 1.8 gather_fusion.1
  16.4 1.8 gather_fusion.2
  18.2 5.4 %collective-permute-start.1 = (bf16[1,1,32,1536]{3,2,1,0:T(8,128)(2,1)S(1)}, bf16[1,1,32,1536]{3,2,1,0:T(8,128)(2,1)S(1)}, u32[]{:S(2)}, u32[]{:S(2)}) collective-permute-start(bf16[1,1,32,1536]{3,2,1,0:T(8,128)(2,1)S(1)} %bitcast.177), channel_id=1, source_target_pairs={{1,0},{2,1},{3,2},{4,3},{5,4},{6,5},{7,6},{8,7},{9,8},{10,9},{11,1... | collective-permute-start | bytes 294920 | tf_op jit(solution)/shard_map/ppermute | solution.py:29
  24.6 3.2 gather_fusion
  31.8 6.9 %collective-permute-done.3 = bf16[96,2048]{1,0:T(8,128)(2,1)S(1)} collective-permute-done((bf16[96,2048]{1,0:T(8,128)(2,1)S(1)}, bf16[96,2048]{1,0:T(8,128)(2,1)S(1)}, u32[]{:S(2)}, u32[]{:S(2)}) %collective-permute-start.3) | collective-permute-done | bytes 393248 | tf_op jit(solution)/shard_map/ppermute | solution.py:14
  41.5 22.8 %collective-permute-done.4 = bf16[192,2048]{1,0:T(8,128)(2,1)S(1)} collective-permute-done((bf16[192,2048]{1,0:T(8,128)(2,1)S(1)}, bf16[192,2048]{1,0:T(8,128)(2,1)S(1)}, u32[]{:S(2)}, u32[]{:S(2)}) %collective-permute-start.4) | collective-permute-done | bytes 786464 | tf_op jit(solution)/shard_map/ppermute | solution.py:14
  68.7 1.6 gather_fusion.4
  75.7 42.6 %collective-permute-done.5 = bf16[384,2048]{1,0:T(8,128)(2,1)} collective-permute-done((bf16[384,2048]{1,0:T(8,128)(2,1)}, bf16[384,2048]{1,0:T(8,128)(2,1)}, u32[]{:S(2)}, u32[]{:S(2)}) %collective-permute-start.5) | collective-permute-done | bytes 1572896 | tf_op jit(solution)/shard_map/ppermute | solution.py:14
  118.3 3.5 %constant_dynamic-update-slice_fusion = (bf16[768,2048]{1,0:T(8,128)(2,1)}, bf16[3072,2048]{1,0:T(8,128)(2,1)}) fusion(bf16[768,2048]{1,0:T(8,128)(2,1)} %get-tuple-element.25, bf16[384,2048]{1,0:T(8,128)(2,1)} %collective-permute-done.5, bf16[3072,2048]{1,0:T(8,128)(2,1)} %get-tuple-element.26), kind=kLoop, calls=%fused_computation.151 | loop fusion | bytes 4718592 | tf_op jit(solution)/shard_map/concatenate | solution.py:13
  122.8 1.6 gather_fusion.5
  125.6 1.6 gather_fusion.6
  127.3 2.1 copy.92
  129.3 1.6 gather_fusion.7
  131.0 2.0 copy.94
  133.0 1.6 gather_fusion.8
  134.7 2.1 copy.96
  142.4 115.9 %collective-permute-done.6 = bf16[768,2048]{1,0:T(8,128)(2,1)} collective-permute-done((bf16[768,2048]{1,0:T(8,128)(2,1)}, bf16[768,2048]{1,0:T(8,128)(2,1)}, u32[]{:S(2)}, u32[]{:S(2)}) %collective-permute-start.6) | collective-permute-done | bytes 3145760 | tf_op jit(solution)/shard_map/ppermute | solution.py:14
  258.3 4.1 %constant_dynamic-update-slice_fusion.11 = bf16[3072,2048]{1,0:T(8,128)(2,1)} fusion(bf16[3072,2048]{1,0:T(8,128)(2,1)} %get-tuple-element.20, bf16[768,2048]{1,0:T(8,128)(2,1)} %collective-permute-done.6), kind=kLoop, calls=%fused_computation.162 | loop fusion | bytes 6291456
  265.6 2.8 constant_dynamic-update-slice_fusion.6
  268.4 4.0 %constant_dynamic-update-slice_fusion.5 = bf16[3072,2048]{1,0:T(8,128)(2,1)} fusion(bf16[3072,2048]{1,0:T(8,128)(2,1)} %constant_dynamic-update-slice_fusion.6, bf16[768,2048]{1,0:T(8,128)(2,1)} %collective-permute-done.6), kind=kLoop, calls=%fused_computation.156 | loop fusion | bytes 6291456 | tf_op jit(solution)/shard_map/jit(_roll_dynamic)/concatenate | solution.py:18
  272.5 5.5 %fusion.67 = f32[128,2048]{0,1:T(8,128)S(1)} fusion(bf16[1536,2048]{1,0:T(8,128)(2,1)} %all-gather.2.cloned.1.call-done, bf16[1,128,1536]{2,1,0:T(8,128)(2,1)S(1)} %add_convert_fusion, f32[1536]{0:T(1024)S(1)} %copy-done.30, f32[128]{0:T(128)S(1)} %add_rsqrt_fusion), kind=kOutput, calls=%fused_computation.92 | convolution fusion | flops 806092800 | bytes 7739904 | tf_op jit(solution)/shard_map/brw,wh->brh/dot_general | solution.py:58
  278.0 11.5 %fusion.26 = (f32[128]{0:T(128)S(1)}, f32[128,1536]{1,0:T(8,128)S(1)}) fusion(bf16[1,128,1536]{2,1,0:T(8,128)(2,1)S(1)} %add_convert_fusion, f32[1536]{0:T(1024)S(1)} %copy-done.30, bf16[1536,2048]{1,0:T(8,128)(2,1)} %all-gather.2.cloned.1.call-done, bf16[3072,2048]{1,0:T(8,128)(2,1)} %constant_dynamic-update-slice_fusion.5, s32[]{:T(128)S(6)} %select_n.78, ...), kind=kOutput, calls=%fused_computation.39 | convolution fusion | flops 1613758336 | bytes 15211012 | tf_op jit(solution)/shard_map/brh,wh->brw/dot_general | solution.py:64
  291.7 3.2 scatter_custom_fusion
  294.9 4.6 %scatter_custom_fusion.1 = f32[193,1536]{1,0:T(8,128)} fusion(f32[193,1536]{1,0:T(8,128)} %scatter_custom_fusion, s32[128]{0:T(128)} %copy-done.71, f32[1,128,1536]{2,1,0:T(8,128)S(1)} %copy.115, f32[1,128,1536]{2,1,0:T(8,128)S(1)} %copy.114, f32[128]{0:T(128)} %get-tuple-element.50, f32[128]{0:T(128)} %get-tuple-element.16, f32[128]{0:T(128)} %get-tuple-element.71), kind=kCustom, calls=%fused_computation.58 | custom fusion | flops 983040 | bytes 2760192 | tf_op jit(solution)/shard_map/scatter-add | solution.py:145
  299.5 4.4 %scatter_custom_fusion.2 = f32[193,1536]{1,0:T(8,128)} fusion(f32[193,1536]{1,0:T(8,128)} %scatter_custom_fusion.1, s32[128]{0:T(128)} %copy-done.70, f32[1,128,1536]{2,1,0:T(8,128)S(1)} %copy.115, f32[1,128,1536]{2,1,0:T(8,128)S(1)} %copy.114, f32[128]{0:T(128)S(1)} %copy-done.65, f32[128]{0:T(128)S(1)} %copy-done.53, f32[128]{0:T(128)S(1)} %copy-done.55), kind=kCustom, calls=%fused_computation.56 | custom fusion | flops 983040 | bytes 2760192 | tf_op jit(solution)/shard_map/scatter-add | solution.py:145
  303.9 4.4 %scatter_custom_fusion.3 = f32[193,1536]{1,0:T(8,128)} fusion(f32[193,1536]{1,0:T(8,128)} %scatter_custom_fusion.2, s32[128]{0:T(128)} %copy-done.69, f32[1,128,1536]{2,1,0:T(8,128)S(1)} %copy.115, f32[1,128,1536]{2,1,0:T(8,128)S(1)} %copy.114, f32[128]{0:T(128)S(1)} %copy-done.63, f32[128]{0:T(128)S(1)} %copy-done.49, f32[128]{0:T(128)S(1)} %copy-done.51), kind=kCustom, calls=%fused_computation.54 | custom fusion | flops 983040 | bytes 2760192 | tf_op jit(solution)/shard_map/scatter-add | solution.py:145
  308.4 4.4 %scatter_custom_fusion.4 = f32[193,1536]{1,0:T(8,128)} fusion(f32[193,1536]{1,0:T(8,128)} %scatter_custom_fusion.3, s32[128]{0:T(128)} %copy-done.68, f32[1,128,1536]{2,1,0:T(8,128)S(1)} %copy.115, f32[1,128,1536]{2,1,0:T(8,128)S(1)} %copy.114, f32[128]{0:T(128)S(1)} %copy-done.61, f32[128]{0:T(128)S(1)} %copy-done.45, f32[128]{0:T(128)S(1)} %copy-done.47), kind=kCustom, calls=%fused_computation.52 | custom fusion | flops 983040 | bytes 2760192 | tf_op jit(solution)/shard_map/scatter-add | solution.py:145
  312.8 4.4 %scatter_custom_fusion.5 = f32[193,1536]{1,0:T(8,128)} fusion(f32[193,1536]{1,0:T(8,128)} %scatter_custom_fusion.4, s32[128]{0:T(128)} %copy-done.67, f32[1,128,1536]{2,1,0:T(8,128)S(1)} %copy.115, f32[1,128,1536]{2,1,0:T(8,128)S(1)} %copy.114, f32[128]{0:T(128)S(1)} %copy-done.59, f32[128]{0:T(128)S(1)} %copy-done.41, f32[128]{0:T(128)S(1)} %copy-done.43), kind=kCustom, calls=%fused_computation.50 | custom fusion | flops 983040 | bytes 2760192 | tf_op jit(solution)/shard_map/scatter-add | solution.py:145
  320.0 10.7 %collective-permute-start.8 = (bf16[1,1,32,1536]{3,2,1,0:T(8,128)(2,1)S(1)}, bf16[1,1,32,1536]{3,2,1,0:T(8,128)(2,1)S(1)}, u32[]{:S(2)}, u32[]{:S(2)}) collective-permute-start(bf16[1,1,32,1536]{3,2,1,0:T(8,128)(2,1)S(1)} %bitcast.172), channel_id=1, source_target_pairs={{1,0},{2,1},{3,2},{4,3},{5,4},{6,5},{7,6},{8,7},{9,8},{10,9},{11,1... | collective-permute-start | bytes 294920 | tf_op jit(solution)/shard_map/ppermute | solution.py:29
  330.7 2.2 collective-permute-done.7
  334.3 1.4 scatter_custom_fusion.7
  (237 shorter events, 36.2 us)
Async XLA Ops:
  6.5 18.0 %copy-start = (f32[1024]{0:T(1024)S(1)}, f32[1024]{0:T(1024)}, u32[]{:S(2)}) copy-start(f32[1024]{0:T(1024)} %param.18) | copy-start | bytes 12292
  6.5 265.9 %all-gather.2.cloned.1.call-start = ((), (), s32[]{:S(2)}) async-start(), calls=%async_computation | async-start | bytes 6488064 | tf_op jit(solution)/shard_map/all_gather | solution.py:121
  7.3 21.1 %collective-permute-start.2 = (bf16[48,2048]{1,0:T(8,128)(2,1)}, bf16[48,2048]{1,0:T(8,128)(2,1)S(1)}, u32[]{:S(2)}, u32[]{:S(2)}) collective-permute-start(bf16[48,2048]{1,0:T(8,128)(2,1)} %param.21), channel_id=1, source_target_pairs={{0,31},{1,0},{2,1},{3,2},{4,3},{5,4},{6,5},{7,6},{8,7},{9,8},{10,9... | collective-permute-start | bytes 589832 | tf_op jit(solution)/shard_map/ppermute | solution.py:14
  14.5 9.0 %copy-start.73 = (s32[32]{0:T(128)}, s32[32]{0:T(128)S(1)}, u32[]{:S(2)}) copy-start(s32[32]{0:T(128)S(1)} %get-tuple-element.59) | copy-start | bytes 388
  14.5 9.0 %copy-start.74 = (s32[32]{0:T(128)}, s32[32]{0:T(128)S(1)}, u32[]{:S(2)}) copy-start(s32[32]{0:T(128)S(1)} %get-tuple-element.60) | copy-start | bytes 388
  16.3 49.6 %collective-permute-start = (bf16[1,1,32,1536]{3,2,1,0:T(8,128)(2,1)S(1)}, bf16[1,1,32,1536]{3,2,1,0:T(8,128)(2,1)S(1)}, u32[]{:S(2)}, u32[]{:S(2)}) collective-permute-start(bf16[1,1,32,1536]{3,2,1,0:T(8,128)(2,1)S(1)} %bitcast.175), channel_id=1, source_target_pairs={{0,1},{1,2},{2,3},{3,4},{4,5},{5,6},{6,7},{7,8},{8,9},{9,10},{10,1... | collective-permute-start | bytes 294920 | tf_op jit(solution)/shard_map/ppermute | solution.py:28
  18.2 47.8 %collective-permute-start.1 = (bf16[1,1,32,1536]{3,2,1,0:T(8,128)(2,1)S(1)}, bf16[1,1,32,1536]{3,2,1,0:T(8,128)(2,1)S(1)}, u32[]{:S(2)}, u32[]{:S(2)}) collective-permute-start(bf16[1,1,32,1536]{3,2,1,0:T(8,128)(2,1)S(1)} %bitcast.177), channel_id=1, source_target_pairs={{1,0},{2,1},{3,2},{4,3},{5,4},{6,5},{7,6},{8,7},{9,8},{10,9},{11,1... | collective-permute-start | bytes 294920 | tf_op jit(solution)/shard_map/ppermute | solution.py:29
  27.8 11.1 %copy-start.69 = (s32[128]{0:T(128)}, s32[128]{0:T(128)S(1)}, u32[]{:S(2)}) copy-start(s32[128]{0:T(128)S(1)} %get-tuple-element.54) | copy-start | bytes 1540
  27.9 37.8 %copy-start.67 = (s32[128]{0:T(128)}, s32[128]{0:T(128)S(1)}, u32[]{:S(2)}) copy-start(s32[128]{0:T(128)S(1)} %get-tuple-element.57) | copy-start | bytes 1540
  27.9 37.8 %copy-start.68 = (s32[128]{0:T(128)}, s32[128]{0:T(128)S(1)}, u32[]{:S(2)}) copy-start(s32[128]{0:T(128)S(1)} %get-tuple-element.58) | copy-start | bytes 1540
  28.4 37.2 %copy-start.12 = (bf16[48,2048]{1,0:T(8,128)(2,1)}, bf16[48,2048]{1,0:T(8,128)(2,1)S(1)}, u32[]{:S(2)}) copy-start(bf16[48,2048]{1,0:T(8,128)(2,1)S(1)} %collective-permute-done.2) | copy-start | bytes 589828
  28.5 10.3 %collective-permute-start.3 = (bf16[96,2048]{1,0:T(8,128)(2,1)S(1)}, bf16[96,2048]{1,0:T(8,128)(2,1)S(1)}, u32[]{:S(2)}, u32[]{:S(2)}) collective-permute-start(bf16[96,2048]{1,0:T(8,128)(2,1)S(1)} %pad_maximum_fusion.9), channel_id=1, source_target_pairs={{0,30},{1,31},{2,0},{3,1},{4,2},{5,3},{6,4},{7,5},{8,6},{9,7},{10,... | collective-permute-start | bytes 1179656 | tf_op jit(solution)/shard_map/ppermute | solution.py:14
  29.2 36.5 %copy-start.22 = (bf16[32,32]{0,1:T(8,128)(2,1)}, bf16[32,32]{0,1:T(8,128)(2,1)S(1)}, u32[]{:S(2)}) copy-start(bf16[32,32]{0,1:T(8,128)(2,1)S(1)} %neg.59) | copy-start | bytes 6148
  29.3 36.4 %copy-start.24 = (bf16[32,32]{0,1:T(8,128)(2,1)}, bf16[32,32]{0,1:T(8,128)(2,1)S(1)}, u32[]{:S(2)}) copy-start(bf16[32,32]{0,1:T(8,128)(2,1)S(1)} %copy.102) | copy-start | bytes 6148
  29.4 9.4 %copy-start.18 = (bf16[32,32]{0,1:T(8,128)(2,1)}, bf16[32,32]{0,1:T(8,128)(2,1)S(1)}, u32[]{:S(2)}) copy-start(bf16[32,32]{0,1:T(8,128)(2,1)S(1)} %copy.99) | copy-start | bytes 6148
  38.8 26.9 %copy-start.7 = (bf16[96,2048]{1,0:T(8,128)(2,1)}, bf16[96,2048]{1,0:T(8,128)(2,1)S(1)}, u32[]{:S(2)}) copy-start(bf16[96,2048]{1,0:T(8,128)(2,1)S(1)} %collective-permute-done.3) | copy-start | bytes 1179652
  38.8 25.4 %collective-permute-start.4 = (bf16[192,2048]{1,0:T(8,128)(2,1)S(1)}, bf16[192,2048]{1,0:T(8,128)(2,1)S(1)}, u32[]{:S(2)}, u32[]{:S(2)}) collective-permute-start(bf16[192,2048]{1,0:T(8,128)(2,1)S(1)} %pad_maximum_fusion.7), channel_id=1, source_target_pairs={{0,28},{1,29},{2,30},{3,31},{4,0},{5,1},{6,2},{7,3},{8,4},{9,5},{1... | collective-permute-start | bytes 2359304 | tf_op jit(solution)/shard_map/ppermute | solution.py:14
  64.3 10.1 %copy-start.5 = (bf16[192,2048]{1,0:T(8,128)(2,1)}, bf16[192,2048]{1,0:T(8,128)(2,1)S(1)}, u32[]{:S(2)}) copy-start(bf16[192,2048]{1,0:T(8,128)(2,1)S(1)} %collective-permute-done.4) | copy-start | bytes 2359300
  65.7 52.7 %collective-permute-start.5 = (bf16[384,2048]{1,0:T(8,128)(2,1)}, bf16[384,2048]{1,0:T(8,128)(2,1)}, u32[]{:S(2)}, u32[]{:S(2)}) collective-permute-start(bf16[384,2048]{1,0:T(8,128)(2,1)} %pad_maximum_fusion), channel_id=1, source_target_pairs={{0,24},{1,25},{2,26},{3,27},{4,28},{5,29},{6,30},{7,31},{8,0},{9,1... | collective-permute-start | bytes 4718600 | tf_op jit(solution)/shard_map/ppermute | solution.py:14
  121.9 136.5 %collective-permute-start.6 = (bf16[768,2048]{1,0:T(8,128)(2,1)}, bf16[768,2048]{1,0:T(8,128)(2,1)}, u32[]{:S(2)}, u32[]{:S(2)}) collective-permute-start(bf16[768,2048]{1,0:T(8,128)(2,1)} %get-tuple-element.19), channel_id=1, source_target_pairs={{0,16},{1,17},{2,18},{3,19},{4,20},{5,21},{6,22},{7,23},{8,24},{9,... | collective-permute-start | bytes 9437192 | tf_op jit(solution)/shard_map/ppermute | solution.py:14
  278.0 12.2 %copy-start.20 = (bf16[32,32]{0,1:T(8,128)(2,1)S(1)}, bf16[32,32]{0,1:T(8,128)(2,1)}, u32[]{:S(2)}) copy-start(bf16[32,32]{0,1:T(8,128)(2,1)} %copy-done.18) | copy-start | bytes 6148
  278.0 12.2 %copy-start.27 = (bf16[32,32]{0,1:T(8,128)(2,1)S(1)}, bf16[32,32]{0,1:T(8,128)(2,1)}, u32[]{:S(2)}) copy-start(bf16[32,32]{0,1:T(8,128)(2,1)} %neg.58) | copy-start | bytes 6148
  278.0 12.2 %copy-start.29 = (bf16[32,32]{0,1:T(8,128)(2,1)S(1)}, bf16[32,32]{0,1:T(8,128)(2,1)}, u32[]{:S(2)}) copy-start(bf16[32,32]{0,1:T(8,128)(2,1)} %copy.98) | copy-start | bytes 6148
  294.9 9.0 %copy-start.49 = (f32[128]{0:T(128)S(1)}, f32[128]{0:T(128)}, u32[]{:S(2)}) copy-start(f32[128]{0:T(128)} %get-tuple-element.14) | copy-start | bytes 1540
  294.9 9.0 %copy-start.51 = (f32[128]{0:T(128)S(1)}, f32[128]{0:T(128)}, u32[]{:S(2)}) copy-start(f32[128]{0:T(128)} %get-tuple-element.73) | copy-start | bytes 1540
  294.9 9.0 %copy-start.63 = (f32[128]{0:T(128)S(1)}, f32[128]{0:T(128)}, u32[]{:S(2)}) copy-start(f32[128]{0:T(128)} %get-tuple-element.48) | copy-start | bytes 1540
  299.5 8.9 %copy-start.45 = (f32[128]{0:T(128)S(1)}, f32[128]{0:T(128)}, u32[]{:S(2)}) copy-start(f32[128]{0:T(128)} %get-tuple-element.13) | copy-start | bytes 1540
  299.5 8.9 %copy-start.47 = (f32[128]{0:T(128)S(1)}, f32[128]{0:T(128)}, u32[]{:S(2)}) copy-start(f32[128]{0:T(128)} %get-tuple-element.74) | copy-start | bytes 1540
  299.5 8.9 %copy-start.61 = (f32[128]{0:T(128)S(1)}, f32[128]{0:T(128)}, u32[]{:S(2)}) copy-start(f32[128]{0:T(128)} %get-tuple-element.47) | copy-start | bytes 1540
  303.9 8.9 %copy-start.41 = (f32[128]{0:T(128)S(1)}, f32[128]{0:T(128)}, u32[]{:S(2)}) copy-start(f32[128]{0:T(128)} %get-tuple-element.12) | copy-start | bytes 1540
  319.9 13.1 %collective-permute-start.7 = (bf16[1,1,32,1536]{3,2,1,0:T(8,128)(2,1)S(1)}, bf16[1,1,32,1536]{3,2,1,0:T(8,128)(2,1)S(1)}, u32[]{:S(2)}, u32[]{:S(2)}) collective-permute-start(bf16[1,1,32,1536]{3,2,1,0:T(8,128)(2,1)S(1)} %bitcast.173), channel_id=1, source_target_pairs={{0,1},{1,2},{2,3},{3,4},{4,5},{5,6},{6,7},{7,8},{8,9},{9,10},{10,1... | collective-permute-start | bytes 294920 | tf_op jit(solution)/shard_map/ppermute | solution.py:28
  320.0 13.0 %collective-permute-start.8 = (bf16[1,1,32,1536]{3,2,1,0:T(8,128)(2,1)S(1)}, bf16[1,1,32,1536]{3,2,1,0:T(8,128)(2,1)S(1)}, u32[]{:S(2)}, u32[]{:S(2)}) collective-permute-start(bf16[1,1,32,1536]{3,2,1,0:T(8,128)(2,1)S(1)} %bitcast.172), channel_id=1, source_target_pairs={{1,0},{2,1},{3,2},{4,3},{5,4},{6,5},{7,6},{8,7},{9,8},{10,9},{11,1... | collective-permute-start | bytes 294920 | tf_op jit(solution)/shard_map/ppermute | solution.py:29
  (53 other events, 146.9 us)
Sparse Core Ops, SparseCore 0:
  10.2 99.5 all-gather.1
